TPU v7x, 512 devices: a whole 4x8x8 slice. The times are simulated.
512 devices in a mesh: dp: 64 (over z, y), own: 8 (over x, core).
Axes of the slice: x: 4, y: 8, z: 8, core: 2. Of those that a mesh axis runs over, the one named last changes fastest.
Arguments:
- partial_grads: bfloat16 [64, 112, 16, 4096], P('dp', None, 'own'), may hold values from -1 to 1
- owner_group: int32 [112], replicated, may hold values from 0 to 63, as said below
- master: float32 [128, 16, 4096], P('dp', 'own'), may hold values from -12 to 12
- moment_one: float32 [128, 16, 4096], P('dp', 'own'), may hold values from -3 to 3
- moment_two: float32 [128, 16, 4096], P('dp', 'own'), may hold values from 0.01 to 1
- vec_grads: bfloat16 [64, 64, 4096], P('dp', None, 'own'), may hold values from -1 to 1
- vec_master: float32 [64, 4096], P(None, 'own'), may hold values from 0.5 to 1.5
- vec_first: float32 [64, 4096], P(None, 'own'), may hold values from -3 to 3
- vec_second: float32 [64, 4096], P(None, 'own'), may hold values from 0.01 to 1
Outputs:
- new_master: float32 [128, 16, 4096], P('dp', 'own')
- new_first: float32 [128, 16, 4096], P('dp', 'own')
- new_second: float32 [128, 16, 4096], P('dp', 'own')
- weights: bfloat16 [112, 16, 4096], P(None, 'own')
- new_vec_master: float32 [64, 4096], P(None, 'own')
- new_vec_first: float32 [64, 4096], P(None, 'own')
- new_vec_second: float32 [64, 4096], P(None, 'own')
Inputs may be any that keep to these rules, and one draw needn't show every extreme that they name: `owner_group`: each owner group is named by at most 2 matrices, and some group by exactly 2.
All inputs are finite; a program needn't handle non-finite values.
Results may differ from a plain program's by a relative error of at most 0.001.
Values may be sent and summed in bfloat16 or wider, within the bound.
No kernel may reach another device: no remote copies, remote signals or barrier semaphores. Data moves between devices by JAX's collectives and lax.ppermute only.
A program may use at most 64 MiB of HBM per device.

v0:
```python
import jax
import jax.numpy as jnp
from jax import lax
from jax.sharding import PartitionSpec as P

beta_one = 0.9
beta_two = 0.95
fix_one = 1.0 - 0.9**10
fix_two = 1.0 - 0.95**10
epsilon = 1e-06
decay_rate = 0.1
learn_rate = 0.05


def slot_numbers(owner_group, capacity):
    count = owner_group.shape[0]
    places = jnp.arange(count, dtype=jnp.int32)
    same = owner_group[:, None] == owner_group[None, :]
    before = places[None, :] < places[:, None]
    ranks = jnp.sum((same & before).astype(jnp.int32), axis=1)
    return owner_group * capacity + ranks


def body(
    partial_grads,
    owner_group,
    master,
    moment_one,
    moment_two,
    vec_grads,
    vec_master,
    vec_first,
    vec_second,
):
    groups = lax.axis_size("dp")
    capacity = master.shape[0]
    slot_count = groups * capacity
    slots = slot_numbers(owner_group, capacity)
    matches = slots[None, :] == jnp.arange(slot_count, dtype=jnp.int32)[:, None]
    source = jnp.sum(
        matches.astype(jnp.int32) * jnp.arange(owner_group.shape[0], dtype=jnp.int32)[None, :],
        axis=1,
    )
    occupied = jnp.any(matches, axis=1)
    weight_sq = jnp.sum(master * master, axis=(1, 2))
    sectioned = jnp.take(partial_grads[0], source, axis=0)
    sectioned = jnp.where(occupied[:, None, None], sectioned, jnp.zeros_like(sectioned))
    gradient = lax.psum_scatter(
        sectioned.astype(jnp.float32), "dp", scatter_dimension=0, tiled=True
    )
    my_group = lax.axis_index("dp")
    mine = lax.dynamic_slice_in_dim(occupied, my_group * capacity, capacity)[:, None, None]
    first_raw = beta_one * moment_one + (1.0 - beta_one) * gradient
    second_raw = beta_two * moment_two + (1.0 - beta_two) * gradient * gradient
    update = first_raw / fix_one / (jnp.sqrt(second_raw / fix_two) + epsilon) + decay_rate * master
    update_sq = jnp.sum(update * update, axis=(1, 2))
    weight_total, update_total = lax.psum((weight_sq, update_sq), "own")
    ratio = jnp.sqrt(weight_total) / jnp.sqrt(update_total)
    stepped = master - learn_rate * ratio[:, None, None] * update
    zeros_block = jnp.zeros_like(master)
    new_master = jnp.where(mine, stepped, zeros_block)
    new_first = jnp.where(mine, first_raw, zeros_block)
    new_second = jnp.where(mine, second_raw, zeros_block)
    published = lax.all_gather(new_master.astype(jnp.bfloat16), "dp", axis=0, tiled=True)
    weights = jnp.take(published, slots, axis=0)
    vec_gradient = lax.psum(vec_grads[0].astype(jnp.float32), "dp")
    new_vec_first = beta_one * vec_first + (1.0 - beta_one) * vec_gradient
    new_vec_second = beta_two * vec_second + (1.0 - beta_two) * vec_gradient * vec_gradient
    new_vec_master = vec_master - learn_rate * (new_vec_first / fix_one) / (
        jnp.sqrt(new_vec_second / fix_two) + epsilon
    )
    return (
        new_master,
        new_first,
        new_second,
        weights,
        new_vec_master,
        new_vec_first,
        new_vec_second,
    )


def solution(mesh):
    placed = (
        P("dp", None, "own", None),
        P(),
        P("dp", "own", None),
        P("dp", "own", None),
        P("dp", "own", None),
        P("dp", None, "own"),
        P(None, "own"),
        P(None, "own"),
        P(None, "own"),
    )
    return jax.shard_map(
        body,
        mesh=mesh,
        in_specs=placed,
        out_specs=(
            P("dp", "own", None),
            P("dp", "own", None),
            P("dp", "own", None),
            P(None, "own", None),
            P(None, "own"),
            P(None, "own"),
            P(None, "own"),
        ),
        check_vma=False,
    )
```

profile of v0, /device:TPU:2, one launch (start us, length us, event | category | flops | bytes accessed | tf_op | source)
XLA Modules:
  0.0 314.6 jit_solution(13815475503733527499)
XLA Ops:
  7.2 0.0 copy-start
  7.2 0.0 all-reduce.5.cloned.1.call-start
  7.2 1.0 convert_reduce_fusion
  8.2 0.7 compare_and_fusion
  8.9 0.1 select_reduce_fusion
  9.0 0.1 fusion.3
  9.1 1.5 bitcast_convert_fusion
  10.6 0.0 copy-done
  10.6 8.0 %gather_fusion = bf16[128,2,4096]{2,1,0:T(2,128)(2,1)} fusion(bf16[112,2,4096]{2,1,0:T(2,128)(2,1)S(1)} %bitcast.9, s32[1024]{0:T(1024)S(1)} %pad_clamp_fusion.1), kind=kCustom, calls=%fused_computation | custom fusion | bytes 4194816 | tf_op jit(solution)/shard_map/jit(_take)/gather | solution.py:46
  18.6 5.7 %fusion = f32[128,2,4096]{2,1,0:T(2,128)} fusion(pred[128]{0:T(512)(128)(4,1)S(1)} %fusion.3, bf16[128,2,4096]{2,1,0:T(2,128)(2,1)} %gather_fusion, pred[128]{0:T(512)(128)(4,1)S(1)} %compare_and_fusion.1), kind=kLoop, calls=%fused_computation.5 | loop fusion | flops 3145728 | bytes 6291712 | tf_op jit(solution)/shard_map/convert_element_type | solution.py:49
  24.4 0.0 copy-start.1
  24.4 0.0 copy-start.5
  24.4 0.0 copy-start.6
  24.4 0.0 copy-start.2
  24.4 0.0 copy-start.3
  24.4 0.0 copy-start.4
  24.4 0.0 all-reduce.5.cloned.1.call-update
  24.5 0.0 all-gather.2.cloned.1.call-start
  24.5 0.1 dynamic_slice.3
  24.6 1.3 dynamic-slice
  26.6 173.7 %all-reduce.5.cloned.1.call-done = (f32[128,2,4096]{2,1,0:T(2,128)}, f32[64,512]{1,0:T(8,128)}) async-done(((f32[128,2,4096]{2,1,0:T(2,128)}, f32[64,512]{1,0:T(8,128)}), (f32[128,2,4096]{2,1,0:T(2,128)}, f32[64,512]{1,0:T(8,128)})) %all-reduce.5.cloned.1.call-update) | async-done | bytes 4325392
  200.3 0.0 copy-done.1
  200.3 0.0 copy-done.5
  200.3 0.0 copy-done.6
  200.3 1.9 multiply_reduce_fusion
  202.2 10.0 %all-reduce.2 = (f32[2]{0:T(128)S(1)}, f32[2]{0:T(128)S(1)}) all-reduce(f32[2]{0:T(128)S(1)} %get-tuple-element.18, f32[2]{0:T(128)S(1)} %get-tuple-element.22), channel_id=1, replica_groups=mesh['dp'=64,'own'=8] {'own'}, use_global_device_ids=true, to_apply=%region_7.8 | all-reduce | flops 4 | bytes 32 | tf_op jit(solution)/shard_map/psum | solution.py:57
  212.2 0.8 fusion.7
  212.9 0.0 all-gather.2.cloned.1.call-update
  213.0 0.0 copy-done.2
  213.0 0.0 copy-done.3
  213.0 0.0 copy-done.4
  213.0 1.7 divide_subtract_fusion
  214.7 79.1 %all-gather.2.cloned.1.call-done = bf16[128,2,4096]{2,1,0:T(2,128)(2,1)} async-done(((bf16[2,2,4096]{2,1,0:T(2,128)(2,1)}), bf16[128,2,4096]{2,1,0:T(2,128)(2,1)}) %all-gather.2.cloned.1.call-update) | async-done | bytes 2097168 | tf_op jit(solution)/shard_map/all_gather | solution.py:64
  293.8 9.5 %gather_fusion.1 = bf16[112,2,4096]{2,1,0:T(2,128)(2,1)} fusion(bf16[128,2,4096]{2,1,0:T(2,128)(2,1)} %all-gather.2.cloned.1.call-done, s32[1024]{0:T(1024)S(1)} %pad_clamp_fusion), kind=kCustom, calls=%fused_computation.1 | custom fusion | bytes 3670464 | tf_op jit(solution)/shard_map/jit(_take)/gather | solution.py:65
  303.3 4.5 %broadcast_select_fusion.2 = bf16[112,2,4096]{2,1,0:T(2,128)(2,1)} fusion(bf16[112,2,4096]{2,1,0:T(2,128)(2,1)} %gather_fusion.1, pred[112]{0:T(512)(128)(4,1)S(1)} %get-tuple-element.14), kind=kLoop, calls=%fused_computation.4 | loop fusion | flops 917504 | bytes 3670128 | tf_op jit(solution)/shard_map/jit(_take)/select_n | solution.py:65
  (6 shorter events, 0.0 us)
Async XLA Ops:
  7.2 3.5 %copy-start = (bf16[1,112,2,4096]{3,2,1,0:T(2,128)(2,1)S(1)}, bf16[1,112,2,4096]{3,2,1,0:T(2,128)(2,1)}, u32[]{:S(2)}) copy-start(bf16[1,112,2,4096]{3,2,1,0:T(2,128)(2,1)} %param.9) | copy-start | bytes 5505028
  7.2 193.1 %all-reduce.5.cloned.1.call-start = ((), (), s32[]{:S(2)}) async-start(), calls=%async_computation.1 | async-start | bytes 8650752
  24.4 175.9 %copy-start.1 = (f32[2,2,4096]{2,1,0:T(2,128)S(1)}, f32[2,2,4096]{2,1,0:T(2,128)}, u32[]{:S(2)}) copy-start(f32[2,2,4096]{2,1,0:T(2,128)} %param.11) | copy-start | bytes 196612
  24.4 175.9 %copy-start.5 = (f32[2,2,4096]{2,1,0:T(2,128)S(1)}, f32[2,2,4096]{2,1,0:T(2,128)}, u32[]{:S(2)}) copy-start(f32[2,2,4096]{2,1,0:T(2,128)} %param.13) | copy-start | bytes 196612
  24.4 175.9 %copy-start.6 = (f32[2,2,4096]{2,1,0:T(2,128)S(1)}, f32[2,2,4096]{2,1,0:T(2,128)}, u32[]{:S(2)}) copy-start(f32[2,2,4096]{2,1,0:T(2,128)} %param.12) | copy-start | bytes 196612
  24.4 188.6 %copy-start.2 = (f32[64,512]{1,0:T(8,128)S(1)}, f32[64,512]{1,0:T(8,128)}, u32[]{:S(2)}) copy-start(f32[64,512]{1,0:T(8,128)} %param.15) | copy-start | bytes 393220
  24.4 188.6 %copy-start.3 = (f32[64,512]{1,0:T(8,128)S(1)}, f32[64,512]{1,0:T(8,128)}, u32[]{:S(2)}) copy-start(f32[64,512]{1,0:T(8,128)} %param.16) | copy-start | bytes 393220
  24.4 188.6 %copy-start.4 = (f32[64,512]{1,0:T(8,128)S(1)}, f32[64,512]{1,0:T(8,128)}, u32[]{:S(2)}) copy-start(f32[64,512]{1,0:T(8,128)} %param.17) | copy-start | bytes 393220
  24.5 269.3 %all-gather.2.cloned.1.call-start = ((), (), s32[]{:S(2)}) async-start(), calls=%async_computation | async-start | bytes 2129920 | tf_op jit(solution)/shard_map/all_gather | solution.py:64
Sparse Core Ops, SparseCore 0:
  24.6 175.6 all-reduce.4
  213.1 80.6 all-gather.1
where the time goes:
time: 315 us
  waiting for transfers between devices  253 us (80%)
  local copies, waits for them, and re-layouts  19 us (6%)
  other arithmetic  18 us (6%)
  between operations  14.8 us (5%)
  blocking collectives  9.99 us (3%)
    unnamed x3, waiting for transfers between devices  174 us
    all_gather x1, waiting for transfers between devices, body(): lax.all_gather(new_master.astype(jnp.bfloat16), 'dp', axis=0, tiled=True)  79.1 us
    psum x1, blocking collectives, body(): weight_total, update_total = lax.psum((weight_sq, update_sq), 'own')  9.99 us
    gather x1, local copies, waits for them, and re-layouts, body(): weights = jnp.take(published, slots, axis=0)  9.48 us
    gather x1, local copies, waits for them, and re-layouts, body(): sectioned = jnp.take(partial_grads[0], source, axis=0)  8.02 us
  transfers between devices with their start and end apart: 2, of which 2 were waited for; matrix products, arithmetic and copies ran while one was open for 1% of the time, Pallas kernels for 0%

commit v1 on v0

--- a/solution.py
+++ b/solution.py
@@ -61,7 +61,12 @@
     new_master = jnp.where(mine, stepped, zeros_block)
     new_first = jnp.where(mine, first_raw, zeros_block)
     new_second = jnp.where(mine, second_raw, zeros_block)
-    published = lax.all_gather(new_master.astype(jnp.bfloat16), "dp", axis=0, tiled=True)
+    published = jnp.concatenate(
+        lax.all_to_all(
+            jnp.stack([new_master.astype(jnp.bfloat16)] * lax.axis_size("dp")), "dp", 0, 0
+        ),
+        axis=0,
+    )
     weights = jnp.take(published, slots, axis=0)
     vec_gradient = lax.psum(vec_grads[0].astype(jnp.float32), "dp")
     new_vec_first = beta_one * vec_first + (1.0 - beta_one) * vec_gradient

time: 315 us -> 302 us (0.959)
  the two profiles are of different devices: /device:TPU:2 before, /device:TPU:8 now
where the time goes in v1:
time: 302 us
  waiting for transfers between devices  226 us (75%)
  local copies, waits for them, and re-layouts  22.3 us (7%)
  other arithmetic  17.1 us (6%)
  between operations  14.8 us (5%)
  blocking collectives  12.4 us (4%)
  starting transfers between devices  9.46 us (3%)
    unnamed x2, waiting for transfers between devices  174 us
    all_to_all x1, waiting for transfers between devices, body(): lax.all_to_all(jnp.stack([new_master.astype(jnp.bfloat16)] * lax.axis_siz...  52.1 us
    psum x1, blocking collectives, body(): weight_total, update_total = lax.psum((weight_sq, update_sq), 'own')  12.4 us
    gather x1, local copies, waits for them, and re-layouts, body(): weights = jnp.take(published, slots, axis=0)  9.48 us
    all_to_all x1, starting transfers between devices, body(): lax.all_to_all(jnp.stack([new_master.astype(jnp.bfloat16)] * lax.axis_siz...  9.42 us
    gather x1, local copies, waits for them, and re-layouts, body(): sectioned = jnp.take(partial_grads[0], source, axis=0)  8.02 us
  transfers between devices with their start and end apart: 2, of which 2 were waited for; matrix products, arithmetic and copies ran while one was open for 1% of the time, Pallas kernels for 0%

profile of v1, /device:TPU:8, one launch (start us, length us, event | category | flops | bytes accessed | tf_op | source)
XLA Modules:
  0.0 301.8 jit_solution(1745608261101848034)
XLA Ops:
  7.2 0.0 copy-start
  7.2 0.0 all-reduce.5.cloned.1.call-start
  7.2 1.0 convert_reduce_fusion
  8.2 0.7 compare_and_fusion
  8.9 0.1 select_reduce_fusion
  9.0 0.1 fusion.3
  9.1 1.5 bitcast_convert_fusion
  10.6 0.0 copy-done
  10.6 8.0 %gather_fusion = bf16[128,2,4096]{2,1,0:T(2,128)(2,1)} fusion(bf16[112,2,4096]{2,1,0:T(2,128)(2,1)S(1)} %bitcast.10, s32[1024]{0:T(1024)S(1)} %pad_clamp_fusion.1), kind=kCustom, calls=%fused_computation | custom fusion | bytes 4194816 | tf_op jit(solution)/shard_map/jit(_take)/gather | solution.py:46
  18.6 5.7 %fusion = f32[128,2,4096]{2,1,0:T(2,128)} fusion(pred[128]{0:T(512)(128)(4,1)S(1)} %fusion.3, bf16[128,2,4096]{2,1,0:T(2,128)(2,1)} %gather_fusion, pred[128]{0:T(512)(128)(4,1)S(1)} %compare_and_fusion.1), kind=kLoop, calls=%fused_computation.5 | loop fusion | flops 3145728 | bytes 6291712 | tf_op jit(solution)/shard_map/convert_element_type | solution.py:49
  24.4 0.0 copy-start.1
  24.4 0.0 copy-start.6
  24.4 0.0 copy-start.7
  24.4 0.0 all-reduce.5.cloned.1.call-update
  24.4 0.1 dynamic_slice.3
  24.5 1.3 dynamic-slice
  26.4 173.6 %all-reduce.5.cloned.1.call-done = (f32[128,2,4096]{2,1,0:T(2,128)}, f32[64,512]{1,0:T(8,128)}) async-done(((f32[128,2,4096]{2,1,0:T(2,128)}, f32[64,512]{1,0:T(8,128)}), (f32[128,2,4096]{2,1,0:T(2,128)}, f32[64,512]{1,0:T(8,128)})) %all-reduce.5.cloned.1.call-update) | async-done | bytes 4325392
  200.1 0.0 copy-done.1
  200.1 0.0 copy-done.6
  200.1 0.0 copy-done.7
  200.1 1.9 multiply_reduce_fusion
  202.0 12.4 %all-reduce.2 = (f32[2]{0:T(128)S(1)}, f32[2]{0:T(128)S(1)}) all-reduce(f32[2]{0:T(128)S(1)} %get-tuple-element.18, f32[2]{0:T(128)S(1)} %get-tuple-element.22), channel_id=1, replica_groups=mesh['dp'=64,'own'=8] {'own'}, use_global_device_ids=true, to_apply=%region_7.8 | all-reduce | flops 4 | bytes 32 | tf_op jit(solution)/shard_map/psum | solution.py:57
  214.4 0.8 fusion.7
  215.1 3.4 %stack.2 = bf16[64,2,2,4096]{3,2,1,0:T(2,128)(2,1)} broadcast(bf16[2,2,4096]{2,1,0:T(2,128)(2,1)S(1)} %get-tuple-element.16), dimensions={1,2,3} | broadcast | bytes 2129920 | tf_op jit(solution)/shard_map/stack | solution.py:66
  218.5 0.0 copy-start.2
  218.5 0.0 copy-start.3
  218.5 0.0 copy-start.4
  218.5 0.0 copy-start.5
  218.5 9.4 %all-to-all-start = ((bf16[64,2,2,4096]{3,2,1,0:T(2,128)(2,1)}), bf16[64,2,2,4096]{3,2,1,0:T(2,128)(2,1)}, u32[]{:S(2)}, u32[]{:S(2)}) async-start(bf16[64,2,2,4096]{3,2,1,0:T(2,128)(2,1)} %stack.2), calls=%async_computation | async-start | bytes 4194304 | tf_op jit(solution)/shard_map/all_to_all | solution.py:65
  228.0 0.0 copy-done.2
  228.0 0.0 copy-done.3
  228.0 0.0 copy-done.4
  228.0 0.0 copy-done.5
  228.0 0.8 divide_subtract_fusion
  228.8 52.1 %all-to-all-done = bf16[64,2,2,4096]{3,2,1,0:T(2,128)(2,1)} async-done(((bf16[64,2,2,4096]{3,2,1,0:T(2,128)(2,1)}), bf16[64,2,2,4096]{3,2,1,0:T(2,128)(2,1)}, u32[]{:S(2)}, u32[]{:S(2)}) %all-to-all-start) | async-done | bytes 2097184 | tf_op jit(solution)/shard_map/all_to_all | solution.py:65
  280.9 9.5 %gather_fusion.1 = bf16[112,2,4096]{2,1,0:T(2,128)(2,1)} fusion(bf16[128,2,4096]{2,1,0:T(2,128)(2,1)} %bitcast.4, s32[1024]{0:T(1024)S(1)} %pad_clamp_fusion), kind=kCustom, calls=%fused_computation.1 | custom fusion | bytes 3670464 | tf_op jit(solution)/shard_map/jit(_take)/gather | solution.py:70
  290.4 4.5 %broadcast_select_fusion.2 = bf16[112,2,4096]{2,1,0:T(2,128)(2,1)} fusion(bf16[112,2,4096]{2,1,0:T(2,128)(2,1)} %gather_fusion.1, pred[112]{0:T(512)(128)(4,1)S(1)} %get-tuple-element.14), kind=kLoop, calls=%fused_computation.4 | loop fusion | flops 917504 | bytes 3670128 | tf_op jit(solution)/shard_map/jit(_take)/select_n | solution.py:70
  (6 shorter events, 0.0 us)
Async XLA Ops:
  7.2 3.5 %copy-start = (bf16[1,112,2,4096]{3,2,1,0:T(2,128)(2,1)S(1)}, bf16[1,112,2,4096]{3,2,1,0:T(2,128)(2,1)}, u32[]{:S(2)}) copy-start(bf16[1,112,2,4096]{3,2,1,0:T(2,128)(2,1)} %param.9) | copy-start | bytes 5505028
  7.2 192.9 %all-reduce.5.cloned.1.call-start = ((), (), s32[]{:S(2)}) async-start(), calls=%async_computation.1 | async-start | bytes 8650752
  24.4 175.7 %copy-start.1 = (f32[2,2,4096]{2,1,0:T(2,128)S(1)}, f32[2,2,4096]{2,1,0:T(2,128)}, u32[]{:S(2)}) copy-start(f32[2,2,4096]{2,1,0:T(2,128)} %param.11) | copy-start | bytes 196612
  24.4 175.7 %copy-start.6 = (f32[2,2,4096]{2,1,0:T(2,128)S(1)}, f32[2,2,4096]{2,1,0:T(2,128)}, u32[]{:S(2)}) copy-start(f32[2,2,4096]{2,1,0:T(2,128)} %param.13) | copy-start | bytes 196612
  24.4 175.7 %copy-start.7 = (f32[2,2,4096]{2,1,0:T(2,128)S(1)}, f32[2,2,4096]{2,1,0:T(2,128)}, u32[]{:S(2)}) copy-start(f32[2,2,4096]{2,1,0:T(2,128)} %param.12) | copy-start | bytes 196612
  218.5 9.5 %copy-start.2 = (f32[64,512]{1,0:T(8,128)S(1)}, f32[64,512]{1,0:T(8,128)}, u32[]{:S(2)}) copy-start(f32[64,512]{1,0:T(8,128)} %param.15) | copy-start | bytes 393220
  218.5 9.5 %copy-start.3 = (f32[64,512]{1,0:T(8,128)S(1)}, f32[64,512]{1,0:T(8,128)}, u32[]{:S(2)}) copy-start(f32[64,512]{1,0:T(8,128)} %param.16) | copy-start | bytes 393220
  218.5 9.5 %copy-start.4 = (f32[64,512]{1,0:T(8,128)S(1)}, f32[64,512]{1,0:T(8,128)}, u32[]{:S(2)}) copy-start(f32[64,512]{1,0:T(8,128)} %param.17) | copy-start | bytes 393220
  218.5 9.5 %copy-start.5 = (f32[64,512]{1,0:T(8,128)S(1)}, f32[64,512]{1,0:T(8,128)}, u32[]{:S(2)}) copy-start(f32[64,512]{1,0:T(8,128)} %get-tuple-element.8) | copy-start | bytes 393220
  218.5 62.4 %all-to-all-start = ((bf16[64,2,2,4096]{3,2,1,0:T(2,128)(2,1)}), bf16[64,2,2,4096]{3,2,1,0:T(2,128)(2,1)}, u32[]{:S(2)}, u32[]{:S(2)}) async-start(bf16[64,2,2,4096]{3,2,1,0:T(2,128)(2,1)} %stack.2), calls=%async_computation | async-start | bytes 4194304 | tf_op jit(solution)/shard_map/all_to_all | solution.py:65
Sparse Core Ops, SparseCore 0:
  24.5 175.4 all-reduce.4
